TPU v7x, 256 devices: a whole 4x4x8 slice. The times are simulated.
256 devices in a mesh: ctx: 32 (over z, y), tp: 8 (over x, core).
Axes of the slice: x: 4, y: 4, z: 8, core: 2. Of those that a mesh axis runs over, the one named last changes fastest.
Arguments:
- tokens: bfloat16 [24576, 4096], P(('ctx', 'tp')), may hold values from -6 to 6
- norm_gain: float32 [4096], replicated, may hold values from 0.1 to 1.9
- w_qkv: bfloat16 [4096, 8192], P('ctx', 'tp'), may hold values from -0.09375 to 0.09375
- w_out: bfloat16 [4096, 4096], P('tp', 'ctx'), may hold values from -0.09375 to 0.09375
- head_gain: float32 [4096], P('tp'), may hold values from 0.1 to 1.9
- input_codes: int32 [8, 24576], P('tp', 'ctx'), may hold values from -4 to 4
- forget_codes: int32 [8, 24576], P('tp', 'ctx'), may hold values from -24 to 4
- forget_bias: float32 [8], P('tp'), may hold values from 3 to 13.5, as said below
- document_begin_flags: int32 [24576], P('ctx'), may hold values 0 or 1
Outputs:
- mixed: bfloat16 [24576, 4096], P(('ctx', 'tp'))
Inputs may be any that keep to these rules, and one draw needn't show every extreme that they name: `forget_bias`: a bias for each head.
All inputs are finite; a program needn't handle non-finite values. No bound on the sum of `document_begin_flags` on one device may be relied on, other than what follows from the above.
Results may differ from a plain program's by a relative error of at most 0.017.
Values may be sent and summed in bfloat16 or wider, within the bound.
A program may use at most 64 MiB of HBM per device.

v0:
```python
import jax
import jax.numpy as jnp
from jax import lax
from jax.sharding import PartitionSpec as P

DK = 256
DV = 512
EPSILON = 1e-06
FORGET_STEP = 0.5
INPUT_STEP = 0.5


def carried_in(shard, axis, combine, identity):
    count, position = (lax.axis_size(axis), lax.axis_index(axis))
    everything = jax.tree.map(
        lambda part, kind: lax.all_gather(part.astype(kind), axis),
        shard,
        (jnp.bfloat16, jnp.bfloat16),
    )
    start = jax.tree.map(
        lambda part, zero: jnp.broadcast_to(jnp.asarray(zero, part.dtype), part.shape),
        shard,
        identity,
    )

    def hop(k, before):
        reached = k < position
        new = combine(
            before, jax.tree.map(lambda part, own: part[k].astype(own.dtype), everything, shard)
        )
        return jax.tree.map(lambda a, b: jnp.where(reached, a, b), new, before)

    return lax.fori_loop(0, count, hop, start)


def rms_rows(embedded_entries, norm_gain):
    token_float = embedded_entries.astype(jnp.float32)
    moment = jnp.mean(token_float * token_float, axis=1, keepdims=True)
    return (token_float * lax.rsqrt(moment + EPSILON) * norm_gain).astype(jnp.bfloat16)


def local_terms(queries, key_rows, values, log_forget, input_gate, starts):
    length = queries.shape[0]
    scaling = queries.shape[1] ** (-0.5)
    segment = jnp.cumsum(starts)
    levels = jnp.cumsum(log_forget)
    position = jnp.arange(length)
    allowed = (position[:, None] >= position[None, :]) & (segment[:, None] == segment[None, :])
    decays = jnp.where(
        allowed,
        jnp.exp(jnp.minimum(levels[:, None] - levels[None, :], 0.0) + input_gate[None, :]),
        0.0,
    )
    scores = jnp.dot(queries, key_rows.T, preferred_element_type=jnp.float32) * scaling
    weights = (scores * decays).astype(jnp.bfloat16)
    inner_part = jnp.dot(weights, values, preferred_element_type=jnp.float32)
    last_level = levels[-1]
    last_seg = segment[-1]
    keeping = jnp.where(segment == last_seg, jnp.exp(last_level - levels + input_gate), 0.0)
    weighted = (key_rows.astype(jnp.float32) * keeping[:, None]).astype(jnp.bfloat16)
    local_state = lax.dot_general(
        weighted, values, (((0,), (0,)), ((), ())), preferred_element_type=jnp.float32
    )
    passing = jnp.where(last_seg == 0, jnp.exp(last_level), 0.0)
    carried = jnp.where(segment == 0, jnp.exp(levels), 0.0) * scaling
    return (inner_part, local_state, passing, carried)


def apply_state(queries, carried, incoming):
    lifted = queries.astype(jnp.float32) * carried[:, None]
    return jnp.dot(
        lifted, incoming, precision=lax.Precision.HIGHEST, preferred_element_type=jnp.float32
    )


def head_norm(head_out, gain):
    centre = jnp.mean(head_out, axis=1, keepdims=True)
    shifted = head_out - centre
    spread = jnp.mean(shifted * shifted, axis=1, keepdims=True)
    return (shifted * lax.rsqrt(spread + EPSILON) * gain).astype(jnp.bfloat16)


def combine(earlier, later):
    return (earlier[0] * later[0], later[0][:, None, None] * earlier[1] + later[1])


def local(
    tokens,
    norm_gain,
    w_qkv,
    w_out,
    head_gain,
    input_codes,
    forget_codes,
    forget_bias,
    document_begin_flags,
):
    normed = rms_rows(tokens, norm_gain)
    every_row_list = lax.all_gather(normed, "tp", axis=0, tiled=True)
    parameter_collection = lax.all_gather(w_qkv, "ctx", axis=0, tiled=True)
    rows_combined = jnp.dot(
        every_row_list, parameter_collection, preferred_element_type=jnp.float32
    )
    rows_combined = rows_combined.astype(jnp.bfloat16)
    heads_here = forget_bias.shape[0]
    stride = 2 * DK + DV
    query_list, inner_list, state_list, passing_list, carried_list = ([], [], [], [], [])
    attention_slot_number = 0
    offset = attention_slot_number * stride
    queries = rows_combined[:, offset : offset + DK]
    key_rows = rows_combined[:, offset + DK : offset + 2 * DK]
    values = rows_combined[:, offset + 2 * DK : offset + stride]
    log_forget = jax.nn.log_sigmoid(
        FORGET_STEP * forget_codes[attention_slot_number].astype(jnp.float32)
        + forget_bias[attention_slot_number]
    )
    input_gate = INPUT_STEP * input_codes[attention_slot_number].astype(jnp.float32)
    inner_part, local_state, passing, carried = local_terms(
        queries, key_rows, values, log_forget, input_gate, document_begin_flags
    )
    query_list.append(queries)
    inner_list.append(inner_part)
    state_list.append(local_state)
    passing_list.append(passing)
    carried_list.append(carried)
    identity = (jnp.ones((heads_here,), jnp.float32), jnp.zeros((heads_here, DK, DV), jnp.float32))
    scanned = carried_in((jnp.stack(passing_list), jnp.stack(state_list)), "ctx", combine, identity)
    incoming = scanned[1]
    attention_slot_number = 0
    head_out = inner_list[attention_slot_number] + apply_state(
        query_list[attention_slot_number],
        carried_list[attention_slot_number],
        incoming[attention_slot_number],
    )
    normed_heads = head_norm(head_out, head_gain)
    out_columns = lax.all_gather(w_out, "ctx", axis=1, tiled=True)
    summed = lax.psum_scatter(
        jnp.dot(normed_heads, out_columns, preferred_element_type=jnp.float32).astype(jnp.bfloat16),
        "tp",
        scatter_dimension=0,
        tiled=True,
    ).astype(jnp.float32)
    return (tokens.astype(jnp.float32) + summed).astype(jnp.bfloat16)


def solution(mesh):
    placed = (
        P(("ctx", "tp"), None),
        P(),
        P("ctx", "tp"),
        P("tp", "ctx"),
        P("tp"),
        P("tp", "ctx"),
        P("tp", "ctx"),
        P("tp"),
        P("ctx"),
    )
    return jax.shard_map(
        local, mesh=mesh, in_specs=placed, out_specs=P(("ctx", "tp"), None), check_vma=False
    )
```

profile of v0, /device:TPU:1, one launch (start us, length us, event | category | flops | bytes accessed | tf_op | source)
XLA Modules:
  0.0 411.1 jit_solution(12727475956866767131)
XLA Ops:
  6.5 1.4 fusion.2
  8.0 2.3 fusion.4
  14.2 1.3 exponential_select_fusion
  15.5 42.6 %all-gather.6.cloned.1.call-done = bf16[768,4096]{1,0:T(8,128)(2,1)} async-done(((bf16[96,4096]{1,0:T(8,128)(2,1)}), bf16[768,4096]{1,0:T(8,128)(2,1)}) %all-gather.6.cloned.1.call-update) | async-done | bytes 6291472 | tf_op jit(solution)/shard_map/all_gather | solution.py:99
  58.1 100.4 %all-gather.8.cloned.1.call-done = bf16[4096,1024]{1,0:T(8,128)(2,1)} async-done(((bf16[128,1024]{1,0:T(8,128)(2,1)}), bf16[4096,1024]{1,0:T(8,128)(2,1)}) %all-gather.8.cloned.1.call-update) | async-done | bytes 8388624 | tf_op jit(solution)/shard_map/all_gather | solution.py:100
  158.5 10.9 %convolution_convert_fusion.1 = bf16[768,1024]{1,0:T(8,128)(2,1)S(1)} fusion(bf16[768,4096]{1,0:T(8,128)(2,1)} %all-gather.6.cloned.1.call-done, bf16[4096,1024]{1,0:T(8,128)(2,1)} %all-gather.8.cloned.1.call-done), kind=kOutput, calls=%fused_computation.10 | convolution fusion | flops 6443237376 | bytes 16252928 | tf_op jit(solution)/shard_map/dot_general | solution.py:101
  169.5 1.3 convolution_convert_fusion.2
  173.5 0.7 dynamic-update-slice
  174.2 57.4 %all-reduce = bf16[32]{0:T(256)(128)(2,1)S(1)} all-reduce(bf16[32]{0:T(256)(128)(2,1)S(1)} %dynamic-update-slice), channel_id=1, replica_groups=mesh['ctx'=32,'tp'=8] {'ctx'}, use_global_device_ids=true, to_apply=%add | all-reduce | flops 32 | bytes 128
  231.6 2.5 fusion.6
  234.2 32.5 %all-gather.12.cloned.1.call-done = bf16[8192,512]{1,0:T(8,128)(2,1)} async-done(((bf16[256,512]{1,0:T(8,128)(2,1)}), bf16[8192,512]{1,0:T(8,128)(2,1)}) %all-gather.12.cloned.1.call-update) | async-done | bytes 8388624 | tf_op jit(solution)/shard_map/all_gather | solution.py:16
  266.7 81.1 %while.14 = (s32[]{:T(128)}, f32[1,256,512]{2,1,0:T(8,128)S(1)}, s32[]{:T(128)}, bf16[32,1]{0,1:T(2,128)(2,1)S(1)}, bf16[32,1,256,512]{3,2,1,0:T(8,128)(2,1)}, /*index=5*/s32[]{:T(128)}, s32[]{:T(128)}) while((s32[]{:T(128)}, f32[1,256,512]{2,1,0:T(8,128)S(1)}, s32[]{:T(128)}, bf16[32,1]{0,1:T(2,128)(2,1)S(1)}, ...), condition=%wide.region_6.7_spmd.clone, body=%wide.region_5.6_spmd.clone.sunk | while | flops 655365 | bytes 1310839 | solution.py:33
  267.9 1.3 fusion.42
  270.5 1.3 fusion.42
  273.0 1.3 fusion.42
  275.5 1.3 fusion.42
  278.1 1.3 fusion.42
  280.6 1.3 fusion.42
  283.1 1.3 fusion.42
  285.7 1.3 fusion.42
  288.2 1.3 fusion.42
  290.7 1.3 fusion.42
  293.3 1.3 fusion.42
  295.8 1.3 fusion.42
  298.3 1.3 fusion.42
  300.9 1.3 fusion.42
  303.4 1.3 fusion.42
  305.9 1.3 fusion.42
  308.5 1.3 fusion.42
  311.0 1.3 fusion.42
  313.5 1.3 fusion.42
  316.1 1.3 fusion.42
  318.6 1.3 fusion.42
  321.1 1.3 fusion.42
  323.7 1.3 fusion.42
  326.2 1.3 fusion.42
  328.8 1.3 fusion.42
  331.3 1.3 fusion.42
  333.8 1.3 fusion.42
  336.4 1.3 fusion.42
  338.9 1.3 fusion.42
  341.4 1.3 fusion.42
  344.0 1.3 fusion.42
  346.5 1.3 fusion.42
  347.8 3.2 fusion.37
  351.7 7.7 %convolution_convert_fusion = bf16[768,4096]{1,0:T(8,128)(2,1)} fusion(bf16[512,4096]{1,0:T(8,128)(2,1)} %all-gather.10.cloned.1.call-done, f32[768,512]{0,1:T(8,128)S(1)} %get-tuple-element.142, f32[512]{0:T(512)S(1)} %copy-done.5, f32[768]{0:T(1024)S(1)} %add_rsqrt_fusion, f32[768]{0:T(1024)S(1)} %broadcast_multiply_fusion), kind=kOutput, calls=%fused_computation.3 | convolution fusion | flops 3225944064 | bytes 12066816 | tf_op jit(solution)/shard_map/dot_general | solution.py:138
  359.5 42.9 %reduce-scatter.2.cloned.1.call-done = bf16[96,4096]{1,0:T(8,128)(2,1)} async-done(((bf16[768,4096]{1,0:T(8,128)(2,1)}), bf16[96,4096]{1,0:T(8,128)(2,1)}) %reduce-scatter.2.cloned.1.call-update) | async-done | bytes 786448 | tf_op jit(solution)/shard_map/reduce_scatter | solution.py:137
  402.4 2.2 fusion.5
  (78 shorter events, 23.9 us)
Async XLA Ops:
  6.5 5.2 %copy-start.4 = (s32[1,768]{1,0:T(1,128)S(1)}, s32[1,768]{1,0:T(1,128)}, u32[]{:S(2)}) copy-start(s32[1,768]{1,0:T(1,128)} %param.17) | copy-start | bytes 9220
  6.5 5.6 %copy-start.2 = (s32[768]{0:T(1024)S(1)}, s32[768]{0:T(1024)}, u32[]{:S(2)}) copy-start(s32[768]{0:T(1024)} %param.19) | copy-start | bytes 9220
  6.5 51.6 %all-gather.6.cloned.1.call-start = ((), (), s32[]{:S(2)}) async-start(), calls=%async_computation.1 | async-start | bytes 7077888 | tf_op jit(solution)/shard_map/all_gather | solution.py:99
  8.0 6.2 %copy-start.3 = (s32[1,768]{1,0:T(1,128)S(1)}, s32[1,768]{1,0:T(1,128)}, u32[]{:S(2)}) copy-start(s32[1,768]{1,0:T(1,128)} %param.16) | copy-start | bytes 9220
  10.3 148.3 %all-gather.8.cloned.1.call-start = ((), (), s32[]{:S(2)}) async-start(), calls=%async_computation.2 | async-start | bytes 8650752 | tf_op jit(solution)/shard_map/all_gather | solution.py:100
  11.0 255.7 %all-gather.12.cloned.1.call-start = ((), (), s32[]{:S(2)}) async-start(), calls=%async_computation.5 | async-start | bytes 8650752 | tf_op jit(solution)/shard_map/all_gather | solution.py:16
  169.5 64.7 %copy-start.1 = (bf16[768,1024]{1,0:T(8,128)(2,1)}, bf16[768,1024]{1,0:T(8,128)(2,1)S(1)}, u32[]{:S(2)}) copy-start(bf16[768,1024]{1,0:T(8,128)(2,1)S(1)} %convolution_convert_fusion.1) | copy-start | bytes 4718596
  169.5 3.3 copy-start.6
  170.8 180.5 %all-gather.10.cloned.1.call-start = ((), (), s32[]{:S(2)}) async-start(), calls=%async_computation.3 | async-start | bytes 4325376 | tf_op jit(solution)/shard_map/all_gather | solution.py:136
  171.4 231.0 %reduce-scatter.2.cloned.1.call-start = ((), (), s32[]{:S(2)}) async-start(), calls=%async_computation.4 | async-start | bytes 7077888 | tf_op jit(solution)/shard_map/reduce_scatter | solution.py:137
  351.0 0.7 copy-start.5
  359.4 42.9 %copy-start = (bf16[96,4096]{1,0:T(8,128)(2,1)S(1)}, bf16[96,4096]{1,0:T(8,128)(2,1)}, u32[]{:S(2)}) copy-start(bf16[96,4096]{1,0:T(8,128)(2,1)} %param.11) | copy-start | bytes 2359300
Sparse Core Ops, SparseCore 0:
  10.4 47.6 all-gather.5
  60.7 97.8 all-gather.7
  170.9 95.7 all-gather.11
  269.0 77.5 all-gather.9
  359.6 42.7 reduce-scatter.1
where the time goes:
time: 413 us; the launch traced here: 411 us
  waiting for transfers between devices  220 us (53%)
  blocking collectives  57.4 us (14%)
  other arithmetic  48.8 us (12%)
  matrix products  25.7 us (6%)
  local copies, waits for them, and re-layouts  22.3 us (5%)
  loops' own time  21.7 us (5%)
  between operations  15.3 us (4%)
    all_gather x1, waiting for transfers between devices, local(): parameter_collection = lax.all_gather(w_qkv, 'ctx', axis=0, tiled=True)  100 us
    unnamed x1, blocking collectives  57.4 us
    reduce_scatter x1, waiting for transfers between devices, local(): lax.psum_scatter(jnp.dot(normed_heads, out_columns, preferred_element_typ...  42.9 us
    all_gather x1, waiting for transfers between devices, local(): every_row_list = lax.all_gather(normed, 'tp', axis=0, tiled=True)  42.6 us
    select_n x32, other arithmetic, hop(): return jax.tree.map(lambda a, b: jnp.where(reached, a, b), new, before)  40.6 us
    all_gather x1, waiting for transfers between devices, carried_in(): lax.all_gather(part.astype(kind), axis)  32.5 us
    another operation x1, loops' own time, carried_in(): return lax.fori_loop(0, count, hop, start)  21.7 us
    dynamic_slice x32, local copies, waits for them, and re-layouts, hop(): part[k].astype(own.dtype)  18.7 us
  transfers between devices with their start and end apart: 5, of which 4 were waited for; matrix products, arithmetic and copies ran while one was open for 17% of the time, Pallas kernels for 0%

commit v1 on v0

--- a/solution.py
+++ b/solution.py
@@ -97,7 +97,8 @@
 ):
     normed = rms_rows(tokens, norm_gain)
     every_row_list = lax.all_gather(normed, "tp", axis=0, tiled=True)
-    parameter_collection = lax.all_gather(w_qkv, "ctx", axis=0, tiled=True)
+    copies = jnp.concatenate([w_qkv] * lax.axis_size("ctx"), axis=0)
+    parameter_collection = lax.all_to_all(copies, "ctx", 0, 0, tiled=True)
     rows_combined = jnp.dot(
         every_row_list, parameter_collection, preferred_element_type=jnp.float32
     )

time: 413 us -> 491 us (1.19)
  waiting for transfers between devices: 220 us -> 260 us
  local copies, waits for them, and re-layouts: 22.3 us -> 40.8 us
  starting transfers between devices: 0.16 us -> 12.5 us
  blocking collectives: 57.4 us -> 66.5 us
    all_to_all x0 -> x1, waiting for transfers between devices: none -> 139 us  [local(): parameter_collection = lax.all_to_all(copies, 'ctx', 0, 0, tiled=True)]
    all_gather x1 -> x0, waiting for transfers between devices: 100 us -> none  [local(): parameter_collection = lax.all_gather(w_qkv, 'ctx', axis=0, tiled=True)]
    unnamed x17 -> x54, local copies, waits for them, and re-layouts: 1.84 us -> 20.5 us
    all_to_all x0 -> x1, starting transfers between devices: none -> 12.3 us  [local(): parameter_collection = lax.all_to_all(copies, 'ctx', 0, 0, tiled=True)]
    unnamed x1, blocking collectives: 57.4 us -> 66.5 us
  transfers between devices with their start and end apart: 5 -> 5, of which waited for: 4 -> 4; matrix products, arithmetic and copies ran while one was open for 17% -> 15% of each run, Pallas kernels for 0% -> 0%
where the time goes in v1:
time: 491 us; the launch traced here: 489 us
  waiting for transfers between devices  260 us (53%)
  blocking collectives  66.5 us (14%)
  other arithmetic  46.4 us (9%)
  local copies, waits for them, and re-layouts  40.8 us (8%)
  matrix products  25.7 us (5%)
  loops' own time  21.7 us (4%)
  between operations  15.4 us (3%)
  starting transfers between devices  12.5 us (3%)
    all_to_all x1, waiting for transfers between devices, local(): parameter_collection = lax.all_to_all(copies, 'ctx', 0, 0, tiled=True)  139 us
    unnamed x1, blocking collectives  66.5 us
    reduce_scatter x1, waiting for transfers between devices, local(): lax.psum_scatter(jnp.dot(normed_heads, out_columns, preferred_element_typ...  43.5 us
    all_gather x1, waiting for transfers between devices, local(): every_row_list = lax.all_gather(normed, 'tp', axis=0, tiled=True)  42.3 us
    select_n x32, other arithmetic, hop(): return jax.tree.map(lambda a, b: jnp.where(reached, a, b), new, before)  40.6 us
    all_gather x1, waiting for transfers between devices, carried_in(): lax.all_gather(part.astype(kind), axis)  33.5 us
    another operation x1, loops' own time, carried_in(): return lax.fori_loop(0, count, hop, start)  21.7 us
    unnamed x54, local copies, waits for them, and re-layouts  20.5 us
  transfers between devices with their start and end apart: 5, of which 4 were waited for; matrix products, arithmetic and copies ran while one was open for 15% of the time, Pallas kernels for 0%

profile of v1, /device:TPU:1, one launch (start us, length us, event | category | flops | bytes accessed | tf_op | source)
XLA Modules:
  0.0 488.6 jit_solution(12271914335880407105)
XLA Ops:
  22.6 3.2 copy-done.1
  25.9 12.3 %all-to-all-start = ((bf16[32,128,1024]{2,1,0:T(8,128)(2,1)}), bf16[32,128,1024]{2,1,0:T(8,128)(2,1)}, u32[]{:S(2)}, u32[]{:S(2)}) async-start(bf16[32,128,1024]{2,1,0:T(8,128)(2,1)} %bitcast.52), calls=%async_computation | async-start | bytes 16777216 | tf_op jit(solution)/shard_map/all_to_all | solution.py:101
  38.5 1.1 fusion.4
  42.7 1.2 exponential_select_fusion
  43.9 42.3 %all-gather.5.cloned.1.call-done = bf16[768,4096]{1,0:T(8,128)(2,1)} async-done(((bf16[96,4096]{1,0:T(8,128)(2,1)}), bf16[768,4096]{1,0:T(8,128)(2,1)}) %all-gather.5.cloned.1.call-update) | async-done | bytes 6291472 | tf_op jit(solution)/shard_map/all_gather | solution.py:99
  86.2 139.5 %all-to-all-done = bf16[32,128,1024]{2,1,0:T(8,128)(2,1)} async-done(((bf16[32,128,1024]{2,1,0:T(8,128)(2,1)}), bf16[32,128,1024]{2,1,0:T(8,128)(2,1)}, u32[]{:S(2)}, u32[]{:S(2)}) %all-to-all-start) | async-done | bytes 8388640 | tf_op jit(solution)/shard_map/all_to_all | solution.py:101
  225.7 10.9 %convolution_convert_fusion.1 = bf16[768,1024]{1,0:T(8,128)(2,1)S(1)} fusion(bf16[768,4096]{1,0:T(8,128)(2,1)} %all-gather.5.cloned.1.call-done, bf16[4096,1024]{1,0:T(8,128)(2,1)} %bitcast.1), kind=kOutput, calls=%fused_computation.10 | convolution fusion | flops 6443237376 | bytes 16252928 | tf_op jit(solution)/shard_map/dot_general | solution.py:102
  236.6 1.3 convolution_convert_fusion.2
  241.4 66.5 %all-reduce = bf16[32]{0:T(256)(128)(2,1)S(1)} all-reduce(bf16[32]{0:T(256)(128)(2,1)S(1)} %dynamic-update-slice), channel_id=1, replica_groups=mesh['ctx'=32,'tp'=8] {'ctx'}, use_global_device_ids=true, to_apply=%add | all-reduce | flops 32 | bytes 128
  307.9 2.5 fusion.6
  310.4 33.5 %all-gather.9.cloned.1.call-done = bf16[8192,512]{1,0:T(8,128)(2,1)} async-done(((bf16[256,512]{1,0:T(8,128)(2,1)}), bf16[8192,512]{1,0:T(8,128)(2,1)}) %all-gather.9.cloned.1.call-update) | async-done | bytes 8388624 | tf_op jit(solution)/shard_map/all_gather | solution.py:16
  344.0 81.1 %while.14 = (s32[]{:T(128)}, f32[1,256,512]{2,1,0:T(8,128)S(1)}, s32[]{:T(128)}, bf16[32,1]{0,1:T(2,128)(2,1)S(1)}, bf16[32,1,256,512]{3,2,1,0:T(8,128)(2,1)}, /*index=5*/s32[]{:T(128)}, s32[]{:T(128)}) while((s32[]{:T(128)}, f32[1,256,512]{2,1,0:T(8,128)S(1)}, s32[]{:T(128)}, bf16[32,1]{0,1:T(2,128)(2,1)S(1)}, ...), condition=%wide.region_6.7_spmd.clone, body=%wide.region_5.6_spmd.clone.sunk | while | flops 655365 | bytes 1310839 | solution.py:33
  345.2 1.3 fusion.42
  347.7 1.3 fusion.42
  350.3 1.3 fusion.42
  352.8 1.3 fusion.42
  355.3 1.3 fusion.42
  357.9 1.3 fusion.42
  360.4 1.3 fusion.42
  362.9 1.3 fusion.42
  365.5 1.3 fusion.42
  368.0 1.3 fusion.42
  370.5 1.3 fusion.42
  373.1 1.3 fusion.42
  375.6 1.3 fusion.42
  378.2 1.3 fusion.42
  380.7 1.3 fusion.42
  383.2 1.3 fusion.42
  385.8 1.3 fusion.42
  388.3 1.3 fusion.42
  390.8 1.3 fusion.42
  393.4 1.3 fusion.42
  395.9 1.3 fusion.42
  398.4 1.3 fusion.42
  401.0 1.3 fusion.42
  403.5 1.3 fusion.42
  406.0 1.3 fusion.42
  408.6 1.3 fusion.42
  411.1 1.3 fusion.42
  413.7 1.3 fusion.42
  416.2 1.3 fusion.42
  418.7 1.3 fusion.42
  421.3 1.3 fusion.42
  423.8 1.3 fusion.42
  425.1 3.2 fusion.37
  428.5 7.8 %convolution_convert_fusion = bf16[768,4096]{1,0:T(8,128)(2,1)} fusion(bf16[512,4096]{1,0:T(8,128)(2,1)} %all-gather.7.cloned.1.call-done, f32[768,512]{0,1:T(8,128)S(1)} %get-tuple-element.142, f32[512]{0:T(512)S(1)} %copy-done.8, f32[768]{0:T(1024)S(1)} %add_rsqrt_fusion, f32[768]{0:T(1024)S(1)} %broadcast_multiply_fusion), kind=kOutput, calls=%fused_computation.3 | convolution fusion | flops 3225944064 | bytes 12066816 | tf_op jit(solution)/shard_map/dot_general | solution.py:139
  436.3 43.5 %reduce-scatter.2.cloned.1.call-done = bf16[96,4096]{1,0:T(8,128)(2,1)} async-done(((bf16[768,4096]{1,0:T(8,128)(2,1)}), bf16[96,4096]{1,0:T(8,128)(2,1)}) %reduce-scatter.2.cloned.1.call-update) | async-done | bytes 786448 | tf_op jit(solution)/shard_map/reduce_scatter | solution.py:138
  479.9 2.2 fusion.5
  (115 shorter events, 39.8 us)
Async XLA Ops:
  6.5 15.6 %copy-start = (bf16[128,1024]{1,0:T(8,128)(2,1)S(1)}, bf16[128,1024]{1,0:T(8,128)(2,1)}, u32[]{:S(2)}) copy-start(bf16[128,1024]{1,0:T(8,128)(2,1)} %param.13) | copy-start | bytes 786436
  22.6 3.2 copy-start.1
  25.8 12.4 %copy-start.2 = (bf16[96,4096]{1,0:T(8,128)(2,1)S(1)}, bf16[96,4096]{1,0:T(8,128)(2,1)}, u32[]{:S(2)}) copy-start(bf16[96,4096]{1,0:T(8,128)(2,1)} %param.11) | copy-start | bytes 2359300
  25.8 12.7 %copy-start.4 = (f32[4096]{0:T(1024)S(1)}, f32[4096]{0:T(1024)}, u32[]{:S(2)}) copy-start(f32[4096]{0:T(1024)} %param.12) | copy-start | bytes 49156
  25.8 14.5 %copy-start.7 = (s32[1,768]{1,0:T(1,128)S(1)}, s32[1,768]{1,0:T(1,128)}, u32[]{:S(2)}) copy-start(s32[1,768]{1,0:T(1,128)} %param.17) | copy-start | bytes 9220
  25.8 15.0 %copy-start.5 = (s32[768]{0:T(1024)S(1)}, s32[768]{0:T(1024)}, u32[]{:S(2)}) copy-start(s32[768]{0:T(1024)} %param.19) | copy-start | bytes 9220
  25.8 16.9 %copy-start.6 = (s32[1,768]{1,0:T(1,128)S(1)}, s32[1,768]{1,0:T(1,128)}, u32[]{:S(2)}) copy-start(s32[1,768]{1,0:T(1,128)} %param.16) | copy-start | bytes 9220
  25.9 199.8 %all-to-all-start = ((bf16[32,128,1024]{2,1,0:T(8,128)(2,1)}), bf16[32,128,1024]{2,1,0:T(8,128)(2,1)}, u32[]{:S(2)}, u32[]{:S(2)}) async-start(bf16[32,128,1024]{2,1,0:T(8,128)(2,1)} %bitcast.52), calls=%async_computation | async-start | bytes 16777216 | tf_op jit(solution)/shard_map/all_to_all | solution.py:101
  38.2 48.0 %all-gather.5.cloned.1.call-start = ((), (), s32[]{:S(2)}) async-start(), calls=%async_computation.2 | async-start | bytes 7077888 | tf_op jit(solution)/shard_map/all_gather | solution.py:99
  39.7 304.3 %all-gather.9.cloned.1.call-start = ((), (), s32[]{:S(2)}) async-start(), calls=%async_computation.5 | async-start | bytes 8650752 | tf_op jit(solution)/shard_map/all_gather | solution.py:16
  225.7 14.3 %copy-start.9 = (u32[256]{0:T(256)S(1)}, u32[256]{0:T(256)}, u32[]{:S(2)}) copy-start(u32[256]{0:T(256)} %constant.65) | copy-start | bytes 3076
  236.6 107.3 %copy-start.3 = (bf16[768,1024]{1,0:T(8,128)(2,1)}, bf16[768,1024]{1,0:T(8,128)(2,1)S(1)}, u32[]{:S(2)}) copy-start(bf16[768,1024]{1,0:T(8,128)(2,1)S(1)} %convolution_convert_fusion.1) | copy-start | bytes 4718596
  237.9 190.6 %all-gather.7.cloned.1.call-start = ((), (), s32[]{:S(2)}) async-start(), calls=%async_computation.3 | async-start | bytes 4325376 | tf_op jit(solution)/shard_map/all_gather | solution.py:137
  238.7 241.2 %reduce-scatter.2.cloned.1.call-start = ((), (), s32[]{:S(2)}) async-start(), calls=%async_computation.4 | async-start | bytes 7077888 | tf_op jit(solution)/shard_map/reduce_scatter | solution.py:138
  310.4 118.1 %copy-start.8 = (f32[512]{0:T(512)S(1)}, f32[512]{0:T(512)}, u32[]{:S(2)}) copy-start(f32[512]{0:T(512)} %param.15) | copy-start | bytes 6148
Sparse Core Ops, SparseCore 0:
  40.8 45.3 all-gather.4
  238.1 105.8 all-gather.8
  346.4 77.5 all-gather.6
  436.5 43.3 reduce-scatter.1
